TPU v7x, 128 devices: a whole 4x4x4 slice. The times are simulated.
128 devices in a mesh: shard: 32 (over y, z_hi, x), tensor: 4 (over z_lo, core).
Axes of the slice: x: 4, y: 4, z: 4 (z_hi: 2, z_lo: 2; z = z_hi * 2 + z_lo), core: 2. Of those that a mesh axis runs over, the one named last changes fastest.
Arguments:
- acts: bfloat16 [32768, 768], P('shard', 'tensor')
- out_grads: bfloat16 [2, 32768, 768], P(None, 'shard', 'tensor')
- sampled_rows: int32 [2, 262144], P(None, 'shard'), may hold values from 0 to 1023
- proj_grad: float32 [768, 768], P(('shard', 'tensor')), may hold values from -600 to 600
- proj_momentum: float32 [768, 768], P(('shard', 'tensor')), may hold values from -6 to 6
- embed_grad: float32 [49152, 768], P(('shard', 'tensor')), may hold values from -36 to 36
- embed_momentum: float32 [49152, 768], P(('shard', 'tensor')), may hold values from -6 to 6
- token_counts: int32 [49152], P(('shard', 'tensor')), may hold values from 0 to 99
Outputs:
- proj_momentum_new: float32 [768, 768], P(('shard', 'tensor'))
- embed_momentum_new: float32 [49152, 768], P(('shard', 'tensor'))
Inputs may be any that keep to these rules, and one draw needn't show every extreme that they name: `sampled_rows`: entry j of a row picks token (j // 8192) * 1024 + value, one of the 1024 tokens of its index of shard; repeats are allowed.
All inputs are finite; a program needn't handle non-finite values.
Results may differ from a plain program's by a relative error of at most 0.0003.
Values may be sent and summed in bfloat16 or wider, within the bound.
No kernel may reach another device: no remote copies, remote signals or barrier semaphores. Data moves between devices by JAX's collectives and lax.ppermute only.
A program may use at most 128 MiB of HBM per device.

v0:
```python
import jax
import jax.numpy as jnp
from jax import lax
from jax.sharding import PartitionSpec as P

D = 768
VOCAB = 49152
SAMPLE = 2048
NS_ITERS = 3
momentum_decay = 0.9
damping_root = 0.5
count_scale = 64.0
highest = lax.Precision.HIGHEST


def per_device(
    acts,
    out_grads,
    sampled_rows,
    proj_grad,
    proj_momentum,
    embed_grad,
    embed_momentum,
    token_counts,
):
    n_shard = lax.axis_size("shard")
    n_tensor = lax.axis_size("tensor")
    devices_all = n_shard * n_tensor
    flat_index = lax.axis_index("shard") * n_tensor + lax.axis_index("tensor")
    width = D
    row_count = width // devices_all
    sample_total = SAMPLE * devices_all
    picked = jnp.stack(
        [
            jnp.take(acts, sampled_rows[0], axis=0),
            jnp.take(out_grads[0], sampled_rows[0], axis=0),
            jnp.take(out_grads[1], sampled_rows[1], axis=0),
        ]
    )
    sampled = lax.all_to_all(picked, "tensor", split_axis=1, concat_axis=2, tiled=True)
    trace_part = jnp.sum(jnp.square(sampled.astype(jnp.float32)), axis=(1, 2))
    factor_rows = (
        lax.psum_scatter(
            jnp.einsum("fsd,fse->dfe", sampled, sampled, preferred_element_type=jnp.float32),
            ("shard", "tensor"),
            scatter_dimension=0,
            tiled=True,
        )
        / sample_total
    )
    frob_part = jnp.sum(factor_rows * factor_rows, axis=(0, 2))
    count_part = jnp.sum(token_counts).astype(jnp.float32)
    frob_total, trace_total, count_total = lax.psum(
        (frob_part, trace_part, count_part), ("shard", "tensor")
    )
    traces = trace_total / sample_total
    ratio = jnp.sqrt(traces[0] / traces[1])
    embed_ratio = jnp.sqrt(count_total / count_scale / VOCAB / (traces[2] / width))
    shifts = jnp.stack([damping_root * ratio, damping_root / ratio, damping_root / embed_ratio])
    norm_sq = frob_total + 2.0 * shifts * traces + width * shifts * shifts
    start_scale = 1.0 / jnp.sqrt(norm_sq)
    row_ids = flat_index * row_count + jnp.arange(row_count, dtype=jnp.int32)
    eye_rows = (jnp.arange(width, dtype=jnp.int32)[None, :] == row_ids[:, None]).astype(
        jnp.float32
    )[:, None, :]
    damped = factor_rows + shifts[None, :, None] * eye_rows
    rows_now = (
        2.0 * start_scale[None, :, None] * eye_rows
        - (start_scale * start_scale)[None, :, None] * damped
    )
    for iteration in range(NS_ITERS):
        inverses = lax.all_gather(rows_now, ("shard", "tensor"), axis=0, tiled=True)
        if iteration < NS_ITERS - 1:
            product = jnp.einsum("rfk,kfj->rfj", damped, inverses, precision=highest)
            rows_now = 2.0 * rows_now - jnp.einsum(
                "rfk,kfj->rfj", product, inverses, precision=highest
            )
    g_inverse = inverses[:, 1, :]
    e_inverse = inverses[:, 2, :]
    a_rows = lax.dynamic_slice_in_dim(inverses[:, 0, :], flat_index * row_count, row_count, 0)
    mixed_rows = jnp.dot(proj_grad, g_inverse, precision=highest)
    update = jnp.dot(
        a_rows,
        lax.all_gather(mixed_rows, ("shard", "tensor"), axis=0, tiled=True),
        precision=highest,
    )
    row_scale = token_counts.astype(jnp.float32) / count_scale + damping_root * embed_ratio
    embed_update = jnp.dot(embed_grad, e_inverse, precision=highest) / row_scale[:, None]
    return (momentum_decay * proj_momentum + update, momentum_decay * embed_momentum + embed_update)


def solution(mesh):
    return jax.shard_map(
        per_device,
        mesh=mesh,
        in_specs=(
            P("shard", "tensor"),
            P(None, "shard", "tensor"),
            P(None, "shard"),
            P(("shard", "tensor"), None),
            P(("shard", "tensor"), None),
            P(("shard", "tensor"), None),
            P(("shard", "tensor"), None),
            P(("shard", "tensor")),
        ),
        out_specs=(P(("shard", "tensor"), None), P(("shard", "tensor"), None)),
        check_vma=False,
    )
```

profile of v0, /device:TPU:1, one launch (start us, length us, event | category | flops | bytes accessed | tf_op | source)
XLA Modules:
  0.0 1483.3 jit_solution(11976387362760375360)
XLA Ops:
  7.2 0.0 copy-start
  7.2 0.0 all-reduce.4.cloned.1.call-start
  7.2 1.0 fusion.62
  8.3 1.2 copy.48
  9.5 1.2 fusion.61
  10.7 0.2 copy.72
  10.9 0.2 copy.73
  11.1 32.9 %gather_fusion.1 = bf16[8192,192]{1,0:T(8,128)(2,1)} fusion(bf16[1024,192]{1,0:T(8,128)(2,1)S(1)} %bitcast.65, s32[8192]{0:T(1024)S(1)} %fusion.50), kind=kCustom, calls=%fused_computation.1.clone | custom fusion | bytes 6324224 | tf_op jit(solution)/shard_map/jit(_take)/gather | solution.py:36
  44.0 32.9 %gather_fusion = bf16[8192,192]{1,0:T(8,128)(2,1)} fusion(bf16[1024,192]{1,0:T(8,128)(2,1)S(1)} %copy.48, s32[8192]{0:T(1024)S(1)} %fusion.50), kind=kCustom, calls=%fused_computation.clone | custom fusion | bytes 6324224 | tf_op jit(solution)/shard_map/jit(_take)/gather | solution.py:35
  76.9 32.9 %gather_fusion.2 = bf16[8192,192]{1,0:T(8,128)(2,1)} fusion(bf16[1024,192]{1,0:T(8,128)(2,1)S(1)} %bitcast.64, s32[8192]{0:T(1024)S(1)} %fusion.51), kind=kCustom, calls=%fused_computation.2.clone | custom fusion | bytes 6324224 | tf_op jit(solution)/shard_map/jit(_take)/gather | solution.py:37
  109.9 0.0 copy-start.1
  109.9 0.0 copy-start.2
  109.9 6.8 select_bitcast_fusion
  116.7 0.0 copy-done.1
  116.7 0.0 copy-done.2
  116.7 4.3 select_bitcast_fusion.2
  121.0 6.2 pad_maximum_fusion
  127.2 17.9 %copy.51 = bf16[3,8192,192]{2,0,1:T(4,128)(2,1)S(1)} copy(bf16[3,8192,192]{2,1,0:T(8,128)(2,1)} %pad_maximum_fusion) | data formatting | bytes 18874368 | tf_op jit(solution)/shard_map/stack | solution.py:33
  145.1 187.7 %all_to_all.18 = bf16[3,8192,192]{2,0,1:T(4,128)(2,1)} all-to-all(bf16[3,8192,192]{2,0,1:T(4,128)(2,1)S(1)} %copy.51), channel_id=1, replica_groups=mesh['shard'=32,'tensor'=4] {'tensor'}, dimensions={1} | all-to-all | bytes 18874368 | tf_op jit(solution)/shard_map/all_to_all | solution.py:40
  332.8 24.3 %copy.53 = bf16[3,2048,4,192]{1,3,2,0:T(8,128)(2,1)} copy(bf16[3,2048,4,192]{3,0,1,2:T(4,128)(2,1)} %bitcast.66) | data formatting | bytes 18874368 | tf_op jit(solution)/shard_map/all_to_all | solution.py:40
  357.0 14.6 convolution_bitcast_fusion
  371.7 11.0 copy.55
  382.7 0.0 copy-start.3
  382.7 0.0 all-reduce.4.cloned.1.call-update
  382.7 0.5 all-gather.6.cloned.1.call-start
  383.2 0.1 copy-done.3
  383.4 0.6 reduce_sum.29
  384.7 26.6 %copy.67 = bf16[3,4,2048,192]{2,1,3,0:T(4,128)(2,1)} copy(bf16[3,4,2048,192]{3,0,2,1:T(4,128)(2,1)} %bitcast.67) | data formatting | bytes 18874368 | tf_op jit(solution)/shard_map/all_to_all | solution.py:40
  411.2 10.6 multiply_reduce_fusion
  421.8 127.8 %all-reduce.4.cloned.1.call-done = f32[768,3,768]{2,1,0:T(4,128)} async-done(((f32[768,3,768]{2,1,0:T(4,128)}), f32[768,3,768]{2,1,0:T(4,128)}) %all-reduce.4.cloned.1.call-update) | async-done | bytes 7077904
  549.6 0.9 constant_dynamic-slice_fusion
  550.5 0.1 multiply_reduce_fusion.1
  550.6 0.1 fusion.54
  550.7 64.2 %all-reduce.1 = (f32[]{:T(128)}, f32[3]{0:T(128)S(1)}, f32[3]{0:T(128)S(1)}) all-reduce(f32[]{:T(128)S(6)} %convert_element_type.18, f32[3]{0:T(128)S(1)} %multiply_reduce_fusion, f32[3]{0:T(128)S(1)} %multiply_reduce_fusion.1), channel_id=1, replica_groups=mesh['shard'=32,'tensor'=4] {'shard','tensor'}, use_global_device_ids=true, to_apply=%region_6.8 | all-reduce | flops 7 | bytes 56 | tf_op jit(solution)/shard_map/psum | solution.py:53
  614.9 0.6 fusion.63
  618.3 0.1 broadcast_multiply_fusion
  618.4 0.1 multiply_subtract_fusion
  618.5 0.7 copy.57
  619.2 0.0 all-gather.6.cloned.1.call-update
  619.2 0.2 all-gather.8.cloned.1.call-start
  619.4 199.9 %all-gather.6.cloned.1.call-done = f32[768,3,768]{2,1,0:T(4,128)} async-done(((f32[6,3,768]{2,1,0:T(4,128)}), f32[768,3,768]{2,1,0:T(4,128)}) %all-gather.6.cloned.1.call-update) | async-done | bytes 7077904 | tf_op jit(solution)/shard_map/all_gather | solution.py:72
  819.3 7.9 fusion.29
  827.2 7.9 fusion.26
  835.1 0.7 copy.60
  835.8 0.0 all-gather.8.cloned.1.call-update
  835.8 0.3 all-gather.10.cloned.1.call-start
  836.1 201.5 %all-gather.8.cloned.1.call-done = f32[768,3,768]{2,1,0:T(4,128)} async-done(((f32[6,3,768]{2,1,0:T(4,128)}), f32[768,3,768]{2,1,0:T(4,128)}) %all-gather.8.cloned.1.call-update) | async-done | bytes 7077904 | tf_op jit(solution)/shard_map/all_gather | solution.py:72
  1037.6 7.9 fusion.38
  1045.5 7.9 fusion.35
  1053.4 0.7 copy.63
  1054.1 0.0 all-gather.10.cloned.1.call-update
  1054.1 0.3 all-gather.12.cloned.1.call-start
  1054.4 201.6 %all-gather.10.cloned.1.call-done = f32[768,3,768]{2,1,0:T(4,128)} async-done(((f32[6,3,768]{2,1,0:T(4,128)}), f32[768,3,768]{2,1,0:T(4,128)}) %all-gather.10.cloned.1.call-update) | async-done | bytes 7077904 | tf_op jit(solution)/shard_map/all_gather | solution.py:72
  1256.0 16.8 %fusion.60 = (f32[768,1,768]{2,1,0:T(1,128)}, f32[768,1,768]{2,1,0:T(1,128)S(1)}, f32[768,1,768]{2,1,0:T(1,128)S(1)}) fusion(f32[768,3,768]{2,1,0:T(4,128)} %all-gather.10.cloned.1.call-done), kind=kLoop, calls=%fused_computation.66 | loop fusion | bytes 14155776 | tf_op jit(solution)/shard_map/slice | solution.py:79
  1272.8 2.7 fusion.41
  1275.5 0.0 all-gather.12.cloned.1.call-update
  1275.5 2.7 copy.64
  1278.2 0.0 copy-done
  1278.2 10.5 fusion.20
  1288.7 2.7 copy.65
  1291.3 0.6 constant_dynamic-slice_fusion.1
  1291.9 179.2 %all-gather.12.cloned.1.call-done = f32[128,6,768]{2,1,0:T(8,128)} async-done(((f32[1,6,768]{2,1,0:T(8,128)}), f32[128,6,768]{2,1,0:T(8,128)}) %all-gather.12.cloned.1.call-update) | async-done | bytes 2359312 | tf_op jit(solution)/shard_map/all_gather | solution.py:84
  1471.1 2.7 reshape.75
  1473.8 2.6 convolution_add_fusion
  (8 shorter events, 0.1 us)
Async XLA Ops:
  7.2 1271.0 %copy-start = (f32[384,768]{1,0:T(8,128)S(1)}, f32[384,768]{1,0:T(8,128)}, u32[]{:S(2)}) copy-start(f32[384,768]{1,0:T(8,128)} %param.15) | copy-start | bytes 3538948
  7.2 542.4 %all-reduce.4.cloned.1.call-start = ((), (), s32[]{:S(2)}) async-start(), calls=%async_computation.5 | async-start | bytes 18874368
  109.9 6.8 copy-start.1
  109.9 6.9 copy-start.2
  382.7 0.7 copy-start.3
  382.7 436.6 %all-gather.6.cloned.1.call-start = ((), (), s32[]{:S(2)}) async-start(), calls=%async_computation.1 | async-start | bytes 9510912 | tf_op jit(solution)/shard_map/all_gather | solution.py:72
  619.2 418.4 %all-gather.8.cloned.1.call-start = ((), (), s32[]{:S(2)}) async-start(), calls=%async_computation.2 | async-start | bytes 9510912 | tf_op jit(solution)/shard_map/all_gather | solution.py:72
  835.8 420.2 %all-gather.10.cloned.1.call-start = ((), (), s32[]{:S(2)}) async-start(), calls=%async_computation.3 | async-start | bytes 9510912 | tf_op jit(solution)/shard_map/all_gather | solution.py:72
  1054.1 417.0 %all-gather.12.cloned.1.call-start = ((), (), s32[]{:S(2)}) async-start(), calls=%async_computation.4 | async-start | bytes 3170304 | tf_op jit(solution)/shard_map/all_gather | solution.py:84
Sparse Core Ops, SparseCore 0:
  382.8 166.7 all-reduce.3
  619.3 199.9 all-gather.5
  835.9 201.5 all-gather.7
  1054.2 201.7 all-gather.9
  1275.6 195.4 all-gather.11
where the time goes:
time: 1490 us; the launch traced here: 1480 us
  waiting for transfers between devices  910 us (61%)
  blocking collectives  252 us (17%)
  local copies, waits for them, and re-layouts  211 us (14%)
  matrix products  62.1 us (4%)
  other arithmetic  29 us (2%)
  between operations  17.8 us (1%)
    all_gather x3, waiting for transfers between devices, per_device(): inverses = lax.all_gather(rows_now, ('shard', 'tensor'), axis=0, tiled=True)  603 us
    all_to_all x1, blocking collectives, per_device(): lax.all_to_all(picked, 'tensor', split_axis=1, concat_axis=2, tiled=True)  188 us
    all_gather x1, waiting for transfers between devices, per_device(): lax.all_gather(mixed_rows, ('shard', 'tensor'), axis=0, tiled=True)  179 us
    unnamed x6, waiting for transfers between devices  128 us
    psum x1, blocking collectives, per_device(): lax.psum((frob_part, trace_part, count_part), ('shard', 'tensor'))  64.2 us
    all_to_all x2, local copies, waits for them, and re-layouts, per_device(): lax.all_to_all(picked, 'tensor', split_axis=1, concat_axis=2, tiled=True)  50.8 us
    gather x1, local copies, waits for them, and re-layouts, per_device(): jnp.take(out_grads[0], sampled_rows[0], axis=0)  32.9 us
    gather x1, local copies, waits for them, and re-layouts, per_device(): jnp.take(out_grads[1], sampled_rows[1], axis=0)  32.9 us
  transfers between devices with their start and end apart: 5, of which 5 were waited for; matrix products, arithmetic and copies ran while one was open for 4% of the time, Pallas kernels for 0%

commit v1 on v0

--- a/solution.py
+++ b/solution.py
@@ -1,3 +1,4 @@
+import functools
 import jax
 import jax.numpy as jnp
 from jax import lax
@@ -11,6 +12,18 @@
 damping_root = 0.5
 count_scale = 64.0
 highest = lax.Precision.HIGHEST
+
+
+def register_the_heads(shard_in, group_axis):
+    return jnp.concatenate(
+        lax.all_to_all(
+            jnp.stack(jnp.split(shard_in, lax.axis_size(group_axis), 1), axis=0), group_axis, 0, 0
+        ),
+        2,
+    )
+
+
+_produce_cells = functools.partial(register_the_heads, group_axis="tensor")
 
 
 def per_device(
@@ -37,7 +50,7 @@
             jnp.take(out_grads[1], sampled_rows[1], axis=0),
         ]
     )
-    sampled = lax.all_to_all(picked, "tensor", split_axis=1, concat_axis=2, tiled=True)
+    sampled = _produce_cells(picked)
     trace_part = jnp.sum(jnp.square(sampled.astype(jnp.float32)), axis=(1, 2))
     factor_rows = (
         lax.psum_scatter(

time: 1490 us -> 1400 us (0.940)
  blocking collectives: 252 us -> 177 us
  local copies, waits for them, and re-layouts: 211 us -> 168 us
  waiting for transfers between devices: 910 us -> 941 us
    all_to_all x1, blocking collectives: 188 us -> 113 us  [register_the_heads(): lax.all_to_all(jnp.stack(jnp.split(shard_in, lax.axis_size(group_axis), 1...]
    all_to_all x2 -> x1, local copies, waits for them, and re-layouts: 50.8 us -> 9.26 us  [register_the_heads(): lax.all_to_all(jnp.stack(jnp.split(shard_in, lax.axis_size(group_axis), 1...]
    unnamed x6, waiting for transfers between devices: 128 us -> 159 us
  transfers between devices with their start and end apart: 5 -> 5, of which waited for: 5 -> 5; matrix products, arithmetic and copies ran while one was open for 4% -> 2% of each run, Pallas kernels for 0% -> 0%
where the time goes in v1:
time: 1400 us; the launch traced here: 1390 us
  waiting for transfers between devices  941 us (67%)
  blocking collectives  177 us (13%)
  local copies, waits for them, and re-layouts  168 us (12%)
  matrix products  62.1 us (4%)
  other arithmetic  27.6 us (2%)
  between operations  17.6 us (1%)
    all_gather x3, waiting for transfers between devices, per_device(): inverses = lax.all_gather(rows_now, ('shard', 'tensor'), axis=0, tiled=True)  603 us
    all_gather x1, waiting for transfers between devices, per_device(): lax.all_gather(mixed_rows, ('shard', 'tensor'), axis=0, tiled=True)  179 us
    unnamed x6, waiting for transfers between devices  159 us
    all_to_all x1, blocking collectives, register_the_heads(): lax.all_to_all(jnp.stack(jnp.split(shard_in, lax.axis_size(group_axis), 1...  113 us
    psum x1, blocking collectives, per_device(): lax.psum((frob_part, trace_part, count_part), ('shard', 'tensor'))  64.2 us
    gather x1, local copies, waits for them, and re-layouts, per_device(): jnp.take(out_grads[0], sampled_rows[0], axis=0)  33.1 us
    gather x1, local copies, waits for them, and re-layouts, per_device(): jnp.take(out_grads[1], sampled_rows[1], axis=0)  33.1 us
    gather x1, local copies, waits for them, and re-layouts, per_device(): jnp.take(acts, sampled_rows[0], axis=0)  33.1 us
  transfers between devices with their start and end apart: 5, of which 5 were waited for; matrix products, arithmetic and copies ran while one was open for 2% of the time, Pallas kernels for 0%

profile of v1, /device:TPU:1, one launch (start us, length us, event | category | flops | bytes accessed | tf_op | source)
XLA Modules:
  0.0 1394.5 jit_solution(2369349266689683021)
XLA Ops:
  7.2 0.0 copy-start
  7.2 0.0 all-reduce.4.cloned.1.call-start
  7.2 1.0 fusion.62
  8.3 1.2 copy.32
  9.5 1.2 fusion.61
  10.7 0.2 copy.53
  10.9 0.2 copy.54
  11.1 33.1 %gather_fusion.1 = bf16[8192,192]{1,0:T(8,128)(2,1)} fusion(bf16[1024,192]{1,0:T(8,128)(2,1)S(1)} %bitcast.71, s32[8192]{0:T(1024)S(1)} %fusion.50), kind=kCustom, calls=%fused_computation.1.clone | custom fusion | bytes 6324224 | tf_op jit(solution)/shard_map/jit(_take)/gather | solution.py:49
  44.2 33.1 %gather_fusion = bf16[8192,192]{1,0:T(8,128)(2,1)} fusion(bf16[1024,192]{1,0:T(8,128)(2,1)S(1)} %copy.32, s32[8192]{0:T(1024)S(1)} %fusion.50), kind=kCustom, calls=%fused_computation.clone | custom fusion | bytes 6324224 | tf_op jit(solution)/shard_map/jit(_take)/gather | solution.py:48
  77.3 33.1 %gather_fusion.2 = bf16[8192,192]{1,0:T(8,128)(2,1)} fusion(bf16[1024,192]{1,0:T(8,128)(2,1)S(1)} %bitcast.70, s32[8192]{0:T(1024)S(1)} %fusion.51), kind=kCustom, calls=%fused_computation.2.clone | custom fusion | bytes 6324224 | tf_op jit(solution)/shard_map/jit(_take)/gather | solution.py:50
  110.4 0.0 copy-start.2
  110.4 6.8 select_bitcast_fusion
  117.2 0.0 copy-done.1
  117.2 0.0 copy-done.2
  117.2 4.3 select_bitcast_fusion.2
  121.5 2.9 pad_maximum_fusion
  124.5 1.1 slice_bitcast_fusion.3
  125.6 6.5 pad_maximum_fusion.1
  132.0 14.9 %copy.35 = bf16[4,3,2048,192]{2,3,1,0:T(8,128)(2,1)} copy(bf16[4,3,2048,192]{3,2,1,0:T(8,128)(2,1)} %pad_maximum_fusion.1) | data formatting | bytes 18874368 | tf_op jit(solution)/shard_map/stack | solution.py:20
  146.9 112.6 %all_to_all.5 = bf16[4,3,2048,192]{2,3,1,0:T(8,128)(2,1)} all-to-all(bf16[4,3,2048,192]{2,3,1,0:T(8,128)(2,1)} %copy.35), channel_id=1, replica_groups=mesh['shard'=32,'tensor'=4] {'tensor'}, dimensions={0} | all-to-all | bytes 18874368 | tf_op jit(solution)/shard_map/all_to_all | solution.py:19
  259.5 9.3 copy.36
  268.8 14.7 %convolution_bitcast_fusion = f32[768,3,768]{0,2,1:T(8,128)} fusion(bf16[3,2048,768]{1,2,0:T(8,128)(2,1)} %bitcast.72), kind=kOutput, calls=%fused_computation.21 | convolution fusion | flops 7247757312 | bytes 16515072 | tf_op jit(solution)/shard_map/fsd,fse->dfe/dot_general | solution.py:57
  283.4 11.0 copy.38
  294.4 0.0 copy-start.3
  294.4 0.0 all-reduce.4.cloned.1.call-update
  294.4 0.5 all-gather.6.cloned.1.call-start
  295.0 0.1 copy-done.3
  295.1 0.6 reduce_sum.29
  296.4 6.0 multiply_reduce_fusion
  302.4 158.7 %all-reduce.4.cloned.1.call-done = f32[768,3,768]{2,1,0:T(4,128)} async-done(((f32[768,3,768]{2,1,0:T(4,128)}), f32[768,3,768]{2,1,0:T(4,128)}) %all-reduce.4.cloned.1.call-update) | async-done | bytes 7077904
  461.1 0.9 constant_dynamic-slice_fusion
  462.0 0.1 multiply_reduce_fusion.1
  462.1 0.1 fusion.54
  462.2 64.2 %all-reduce.1 = (f32[]{:T(128)}, f32[3]{0:T(128)S(1)}, f32[3]{0:T(128)S(1)}) all-reduce(f32[]{:T(128)S(6)} %convert_element_type.18, f32[3]{0:T(128)S(1)} %multiply_reduce_fusion, f32[3]{0:T(128)S(1)} %multiply_reduce_fusion.1), channel_id=1, replica_groups=mesh['shard'=32,'tensor'=4] {'shard','tensor'}, use_global_device_ids=true, to_apply=%region_6.8 | all-reduce | flops 7 | bytes 56 | tf_op jit(solution)/shard_map/psum | solution.py:66
  526.4 0.6 fusion.63
  529.7 0.1 broadcast_multiply_fusion
  529.8 0.1 multiply_subtract_fusion
  529.9 0.7 copy.40
  530.6 0.0 all-gather.6.cloned.1.call-update
  530.6 0.0 all-gather.8.cloned.1.call-start
  530.6 200.1 %all-gather.6.cloned.1.call-done = f32[768,3,768]{2,1,0:T(4,128)} async-done(((f32[6,3,768]{2,1,0:T(4,128)}), f32[768,3,768]{2,1,0:T(4,128)}) %all-gather.6.cloned.1.call-update) | async-done | bytes 7077904 | tf_op jit(solution)/shard_map/all_gather | solution.py:85
  730.7 7.9 fusion.29
  738.6 7.9 fusion.26
  746.6 0.7 copy.43
  747.2 0.0 all-gather.8.cloned.1.call-update
  747.2 0.2 all-gather.10.cloned.1.call-start
  747.5 201.5 %all-gather.8.cloned.1.call-done = f32[768,3,768]{2,1,0:T(4,128)} async-done(((f32[6,3,768]{2,1,0:T(4,128)}), f32[768,3,768]{2,1,0:T(4,128)}) %all-gather.8.cloned.1.call-update) | async-done | bytes 7077904 | tf_op jit(solution)/shard_map/all_gather | solution.py:85
  949.0 7.9 fusion.38
  956.9 7.9 fusion.35
  964.8 0.7 copy.46
  965.5 0.0 all-gather.10.cloned.1.call-update
  965.5 0.3 all-gather.12.cloned.1.call-start
  965.8 201.6 %all-gather.10.cloned.1.call-done = f32[768,3,768]{2,1,0:T(4,128)} async-done(((f32[6,3,768]{2,1,0:T(4,128)}), f32[768,3,768]{2,1,0:T(4,128)}) %all-gather.10.cloned.1.call-update) | async-done | bytes 7077904 | tf_op jit(solution)/shard_map/all_gather | solution.py:85
  1167.4 16.8 %fusion.60 = (f32[768,1,768]{2,1,0:T(1,128)}, f32[768,1,768]{2,1,0:T(1,128)S(1)}, f32[768,1,768]{2,1,0:T(1,128)S(1)}) fusion(f32[768,3,768]{2,1,0:T(4,128)} %all-gather.10.cloned.1.call-done), kind=kLoop, calls=%fused_computation.71 | loop fusion | bytes 14155776 | tf_op jit(solution)/shard_map/slice | solution.py:92
  1184.2 2.7 fusion.41
  1186.9 0.0 all-gather.12.cloned.1.call-update
  1186.9 2.7 copy.47
  1189.6 0.0 copy-done
  1189.6 10.5 fusion.20
  1200.1 2.7 copy.48
  1202.8 0.6 constant_dynamic-slice_fusion.1
  1203.4 179.2 %all-gather.12.cloned.1.call-done = f32[128,6,768]{2,1,0:T(8,128)} async-done(((f32[1,6,768]{2,1,0:T(8,128)}), f32[128,6,768]{2,1,0:T(8,128)}) %all-gather.12.cloned.1.call-update) | async-done | bytes 2359312 | tf_op jit(solution)/shard_map/all_gather | solution.py:97
  1382.5 2.7 reshape.83
  1385.2 2.6 convolution_add_fusion
  (9 shorter events, 0.1 us)
Async XLA Ops:
  7.2 1182.4 %copy-start = (f32[384,768]{1,0:T(8,128)S(1)}, f32[384,768]{1,0:T(8,128)}, u32[]{:S(2)}) copy-start(f32[384,768]{1,0:T(8,128)} %param.15) | copy-start | bytes 3538948
  7.2 453.9 %all-reduce.4.cloned.1.call-start = ((), (), s32[]{:S(2)}) async-start(), calls=%async_computation.5 | async-start | bytes 18874368
  110.4 6.8 copy-start.1
  110.4 6.9 copy-start.2
  294.4 0.7 copy-start.3
  294.4 436.2 %all-gather.6.cloned.1.call-start = ((), (), s32[]{:S(2)}) async-start(), calls=%async_computation.1 | async-start | bytes 9510912 | tf_op jit(solution)/shard_map/all_gather | solution.py:85
  530.6 418.4 %all-gather.8.cloned.1.call-start = ((), (), s32[]{:S(2)}) async-start(), calls=%async_computation.2 | async-start | bytes 9510912 | tf_op jit(solution)/shard_map/all_gather | solution.py:85
  747.2 420.2 %all-gather.10.cloned.1.call-start = ((), (), s32[]{:S(2)}) async-start(), calls=%async_computation.3 | async-start | bytes 9510912 | tf_op jit(solution)/shard_map/all_gather | solution.py:85
  965.5 417.0 %all-gather.12.cloned.1.call-start = ((), (), s32[]{:S(2)}) async-start(), calls=%async_computation.4 | async-start | bytes 3170304 | tf_op jit(solution)/shard_map/all_gather | solution.py:97
Sparse Core Ops, SparseCore 0:
  294.6 166.4 all-reduce.3
  530.7 199.9 all-gather.5
  747.4 201.5 all-gather.7
  965.6 201.7 all-gather.9
  1187.1 195.4 all-gather.11
